TPU v7x, 32 devices: a whole 2x2x4 slice. The times are simulated.
32 devices in a mesh: grp: 8 (over z, x), ulys: 4 (over y, core).
Axes of the slice: x: 2, y: 2, z: 4, core: 2. Of those that a mesh axis runs over, the one named last changes fastest.
Arguments:
- query_in: bfloat16 [4096, 2048], P(('grp', 'ulys')), may hold values from -3 to 3
- key_in: bfloat16 [4096, 2048], P(('grp', 'ulys')), may hold values from -3 to 3
- value_in: bfloat16 [4096, 2048], P(('grp', 'ulys')), may hold values from -6 to 6
- grad_out: bfloat16 [4096, 2048], P(('grp', 'ulys')), may hold values from -6 to 6
- fwd_out: bfloat16 [4096, 2048], P(('grp', 'ulys')), may hold values from -6 to 6
- log_norm: float32 [4096, 32], P(('grp', 'ulys')), may hold values from 3 to 5
- sample_len: int32 [8, 4], P('grp'), may hold values from 1 to 256, 512 in all within a row
- plan_offset: int32 [8, 4], P('grp'), may hold values from -1 to 1, as said below
Outputs:
- grad_query: bfloat16 [4096, 2048], P(('grp', 'ulys'))
- grad_key: bfloat16 [4096, 2048], P(('grp', 'ulys'))
- grad_value: bfloat16 [4096, 2048], P(('grp', 'ulys'))
Inputs may be any that keep to these rules, and one draw needn't show every extreme that they name: `sample_len`: row g lists the sample lengths of pack g; it sums to 512 and its largest entry is 256. `plan_offset`: entry [g, u] = d names block (g + d, u) of an existing group, and entry [g + d, u] is -d, so each column is a permutation of the groups made of swaps of neighbours.
All inputs are finite; a program needn't handle non-finite values.
Results may differ from a plain program's by a relative error of at most 0.012.
Values may be sent and summed in bfloat16 or wider, within the bound.
A program may use at most 128 MiB of HBM per device.

v0:
```python
import functools

import jax
import jax.numpy as jnp
import numpy as np
from jax import lax
from jax.experimental import pallas as pl
from jax.experimental.pallas import tpu as pltpu
from jax.sharding import PartitionSpec as P

MESH = pl.DeviceIdType.MESH
LANES = 128
NT = (((1,), (1,)), ((), ()))
TN = (((0,), (0,)), ((), ()))


def swap_halves(x, low, half):
    return jnp.where(low, pltpu.roll(x, LANES - half, 1), pltpu.roll(x, half, 1))


def kernel(
    n, groups, head_dim,
    freq_ref, len_ref, plan_ref, lse_ref, q_ref, k_ref, v_ref, d_ref, f_ref,
    oq_ref, ok_ref, ov_ref,
    stage, in_buf, f_vm, stat_out, stat_in, stat, cos_t, sin_t, bias,
    qs, kr, dq, grads, home, pair, relay,
    in_send, in_recv, st_send, st_recv, y_send, y_recv, x_send, x_recv, z_send, z_recv,
    loc_sem, df_sem,
):
    g = lax.axis_index("grp")
    me = lax.axis_index("ulys")
    heads_all, rows = lse_ref.shape
    heads = heads_all // n
    chunks = in_buf.shape[0]
    width = chunks * LANES
    per_chunk = LANES // head_dim
    half = head_dim // 2
    group_rows = n * rows
    blocks = n * chunks
    inputs = (q_ref, k_ref, v_ref, d_ref)

    even = lax.rem(g, 2) == 0
    partner = jnp.where(even, g + 1, g - 1)
    up, down = g + 2, g - 2
    has_up, has_down = up < groups, down >= 0
    z_to = jnp.where(even, up, down)
    has_to = jnp.where(even, up < groups, down >= 0)
    has_from = jnp.where(even, down >= 0, up < groups)

    barrier = pltpu.get_barrier_semaphore()
    near_w = jnp.where(lax.rem(me, 2) == 0, me + 1, me - 1)
    far = [lax.rem(near_w - lax.rem(near_w, 2) + o, n) for o in range(2, n)]
    others = far + [near_w]
    for w in others:
        pl.semaphore_signal(barrier, inc=1, device_id=(g, w), device_id_type=MESH)
    pl.semaphore_signal(barrier, inc=1, device_id=(partner, me), device_id_type=MESH)

    @pl.when(has_up)
    def _():
        pl.semaphore_signal(barrier, inc=1, device_id=(up, me), device_id_type=MESH)

    @pl.when(has_down)
    def _():
        pl.semaphore_signal(barrier, inc=1, device_id=(down, me), device_id_type=MESH)

    def load(p, t, w):
        return pltpu.make_async_copy(
            inputs[t].at[:, pl.ds(pl.multiple_of(w * width + p * LANES, LANES), LANES)],
            stage.at[p, w, t],
            loc_sem.at[p, t, w],
        )

    for p in range(chunks):
        for w in far + [near_w, me]:
            for t in range(4):
                load(p, t, w).start()
    copy_f = pltpu.make_async_copy(f_ref, f_vm, df_sem)
    copy_f.start()

    pl.semaphore_wait(barrier, n + has_up.astype(jnp.int32) + has_down.astype(jnp.int32))

    def in_copy(p, w, src):
        return pltpu.make_async_remote_copy(
            src_ref=stage.at[p, w],
            dst_ref=in_buf.at[p, src],
            send_sem=in_send.at[p, w],
            recv_sem=in_recv.at[p, src],
            device_id=(g, w),
            device_id_type=MESH,
        )

    def stat_copy(w, src):
        return pltpu.make_async_remote_copy(
            src_ref=stat_out.at[w], dst_ref=stat_in.at[src],
            send_sem=st_send.at[w], recv_sem=st_recv.at[src],
            device_id=(g, w), device_id_type=MESH,
        )

    def y_copy(p, w, src):
        return pltpu.make_async_remote_copy(
            src_ref=grads.at[p, w], dst_ref=home.at[src * chunks + p],
            send_sem=y_send.at[p, w], recv_sem=y_recv.at[p, src],
            device_id=(g, w), device_id_type=MESH,
        )

    def x_copy(b):
        return pltpu.make_async_remote_copy(
            src_ref=home.at[b], dst_ref=pair.at[b],
            send_sem=x_send.at[b], recv_sem=x_recv.at[b],
            device_id=(partner, me), device_id_type=MESH,
        )

    def z_copy(b):
        return pltpu.make_async_remote_copy(
            src_ref=pair.at[b], dst_ref=relay.at[b],
            send_sem=z_send.at[b], recv_sem=z_recv.at[b],
            device_id=(z_to, me), device_id_type=MESH,
        )

    for p in range(chunks):
        for w in others:
            for t in range(4):
                load(p, t, w).wait()
            if p == 0:
                in_copy(p, w, me).start()
        for t in range(4):
            load(p, t, me).wait()

    copy_f.wait()
    cols = f_vm.shape[1]
    d_full = jnp.concatenate([stage[p, w, 3] for w in range(n) for p in range(chunks)], axis=1)
    prod = d_full.astype(jnp.float32) * f_vm[...].astype(jnp.float32)
    high = prod.astype(jnp.bfloat16)
    rest = (prod - high.astype(jnp.float32)).astype(jnp.bfloat16)
    owner = lax.broadcasted_iota(jnp.int32, (heads_all, cols), 1) - head_dim * lax.broadcasted_iota(
        jnp.int32, (heads_all, cols), 0
    )
    pick = jnp.where((owner >= 0) & (owner < head_dim), 1.0, 0.0).astype(jnp.bfloat16)
    delta = lax.dot_general(pick, high, NT, preferred_element_type=jnp.float32)
    delta += lax.dot_general(pick, rest, NT, preferred_element_type=jnp.float32)
    lse = lse_ref[...]
    for w in range(n):
        stat_out[w, 0] = lse[w * heads:(w + 1) * heads]
        stat_out[w, 1] = delta[w * heads:(w + 1) * heads]
    for w in others:
        stat_copy(w, me).start()
    stat_in[me] = stat_out[me]

    lengths = [len_ref[0, s] for s in range(len_ref.shape[1])]
    ends = []
    for s, length in enumerate(lengths):
        ends.append(length if s == 0 else ends[-1] + length)
    lane = lax.broadcasted_iota(jnp.int32, (rows, LANES), 1)
    low = lax.rem(lane, head_dim) < half

    def segments(index):
        return sum((index >= e).astype(jnp.int32) for e in ends)

    seg_i = segments(lax.broadcasted_iota(jnp.int32, (1, group_rows), 1))

    def tables(w, carry):
        row = lax.broadcasted_iota(jnp.int32, (rows, LANES), 0) + w * rows
        start = sum(jnp.where(row >= e, c, 0) for e, c in zip(ends, lengths))
        angle = (row - start).astype(jnp.float32) * freq_ref[...]
        cos_t[w] = jnp.cos(angle)
        sine = jnp.sin(angle)
        sin_t[w] = jnp.where(low, -sine, sine)
        seg_j = segments(lax.broadcasted_iota(jnp.int32, (rows, 1), 0) + w * rows)
        bias[w] = jnp.where(seg_j == seg_i, 0.0, -1e30)
        return carry

    lax.fori_loop(0, n, tables, 0)

    for w in others:
        stat_copy(w, w).wait_recv()
    for w in range(n):
        for s in range(2):
            stat[s, :, w * rows:(w + 1) * rows] = stat_in[w, s]

    head_of = lax.broadcasted_iota(jnp.int32, (1, LANES), 1) // head_dim

    def step(p, carry):
        @pl.when(p < chunks - 1)
        def _():
            for w in others:
                in_copy(p, w, me).wait_send()
                in_copy(p + 1, w, me).start()

        in_buf[p, me] = stage[p, me]
        for w in others:
            in_copy(p, w, w).wait_recv()

        def rope(w, c):
            cosv, sinv = cos_t[w], sin_t[w]
            at = pl.ds(pl.multiple_of(w * rows, rows), rows)
            for t, out in ((0, qs), (1, kr)):
                x = in_buf[p, w, t].astype(jnp.float32)
                y = (x * cosv + swap_halves(x, low, half) * sinv).astype(jnp.bfloat16)
                out[at, :] = y * 0.125 if t == 0 else y
            return c

        lax.fori_loop(0, n, rope, 0)
        dq[...] = jnp.zeros_like(dq)

        def keys(w, c):
            k_blk = kr[pl.ds(pl.multiple_of(w * rows, rows), rows), :]
            v_blk = in_buf[p, w, 2]
            q_all = qs[...]
            d_all = in_buf[p, :, 3].reshape(group_rows, LANES)
            gv = jnp.zeros((rows, LANES), jnp.float32)
            gk = jnp.zeros((rows, LANES), jnp.float32)
            ds_list, k_list = [], []
            for a in range(per_chunk):
                mine = head_of == a
                q_a = jnp.where(mine, q_all, 0)
                d_a = jnp.where(mine, d_all, 0)
                k_list.append(jnp.where(mine, k_blk, 0))
                h = pl.ds(p * per_chunk + a, 1)
                s = lax.dot_general(k_blk, q_a, NT, preferred_element_type=jnp.float32)
                prob = jnp.exp(s + bias[w] - stat[0, h, :])
                dp = lax.dot_general(v_blk, d_a, NT, preferred_element_type=jnp.float32)
                ds = (prob * (dp - stat[1, h, :])).astype(jnp.bfloat16)
                gv += jnp.dot(prob.astype(jnp.bfloat16), d_a, preferred_element_type=jnp.float32)
                gk += jnp.dot(ds, q_a, preferred_element_type=jnp.float32)
                ds_list.append(ds)
            ds_all = jnp.concatenate(ds_list, axis=0)
            k_all = jnp.concatenate(k_list, axis=0)
            dq[...] += lax.dot_general(ds_all, k_all, TN, preferred_element_type=jnp.float32)
            grads[p, w, 1] = (gk * cos_t[w] - swap_halves(gk, low, half) * sin_t[w]).astype(jnp.bfloat16)
            grads[p, w, 2] = gv.astype(jnp.bfloat16)
            return c

        lax.fori_loop(0, n, keys, 0)

        def finish(w, c):
            x = dq[pl.ds(pl.multiple_of(w * rows, rows), rows), :] * 0.125
            grads[p, w, 0] = (x * cos_t[w] - swap_halves(x, low, half) * sin_t[w]).astype(jnp.bfloat16)
            return c

        lax.fori_loop(0, n, finish, 0)
        for w in others:
            y_copy(p, w, me).start()
        home[me * chunks + p] = grads[p, me]
        x_copy(me * chunks + p).start()

        for lag, act, sources in events:
            @pl.when(p >= lag)
            def _(lag=lag, act=act, sources=sources):
                act(p - lag, sources)

        return carry

    def pass_on(p, sources):
        for w in sources:
            y_copy(p, w, w).wait_recv()
            x_copy(w * chunks + p).start()

    def pass_relay(p, sources):
        for w in sources:
            b = w * chunks + p
            x_copy(b).wait_recv()

            @pl.when(has_to)
            def _():
                z_copy(b).start()

    events = (
        (0, pass_on, [near_w]),
        (1, pass_on, far),
        (1, pass_relay, [me, near_w]),
        (2, pass_relay, far),
    )

    def drain(p):
        for lag, act, sources in events:
            if 0 <= p - lag < chunks:
                act(p - lag, sources)

    @pl.when(jnp.logical_not(has_from))
    def _():
        relay[...] = jnp.zeros_like(relay)

    lax.fori_loop(0, chunks, step, 0)
    drain(chunks)

    offset = jnp.full((rows, LANES), plan_ref[0, me], jnp.int32)
    toward = jnp.where(even, 1, -1)
    stay, near = offset == 0, offset == toward

    def deliver(b):
        @pl.when(has_from)
        def _():
            z_copy(b).wait_recv()

        at = pl.ds(pl.multiple_of(b * LANES, LANES), LANES)
        for t, out in enumerate((oq_ref, ok_ref, ov_ref)):
            out[:, at] = jnp.where(stay, home[b, t], jnp.where(near, pair[b, t], relay[b, t]))

    def deliver_near(p, c):
        for w in (me, near_w):
            deliver(w * chunks + p)
        return c

    def deliver_far(p, c):
        for w in far:
            deliver(w * chunks + p)
        return c

    lax.fori_loop(0, chunks, deliver_near, 0)
    drain(chunks + 1)
    lax.fori_loop(0, chunks, deliver_far, 0)

    for p in range(chunks):
        for w in others:
            y_copy(p, w, me).wait_send()
    for w in others:
        in_copy(chunks - 1, w, me).wait_send()
        stat_copy(w, me).wait_send()

    def sent(b, c):
        x_copy(b).wait_send()

        @pl.when(has_to)
        def _():
            z_copy(b).wait_send()

        return c

    lax.fori_loop(0, blocks, sent, 0)


def per_device(n, groups, query_in, key_in, value_in, grad_out, fwd_out, log_norm, sample_len, plan_offset):
    rows, cols = query_in.shape
    heads_all = log_norm.shape[1]
    head_dim = cols // heads_all
    half = head_dim // 2
    chunks = cols // n // LANES
    heads = heads_all // n
    group_rows = n * rows
    blocks = n * chunks
    freq = np.power(10000.0, -np.arange(half) / half).astype(np.float32)
    freq = jnp.asarray(np.tile(freq, LANES // half)[None, :])
    bf16, f32 = jnp.bfloat16, jnp.float32
    vmem = pl.BlockSpec(memory_space=pltpu.VMEM)
    smem = pl.BlockSpec(memory_space=pltpu.SMEM)
    hbm = pl.BlockSpec(memory_space=pl.ANY)
    dma = pltpu.SemaphoreType.DMA
    return pl.pallas_call(
        functools.partial(kernel, n, groups, head_dim),
        out_shape=(pltpu.VMEM((rows, cols), bf16),) * 3,
        in_specs=[vmem, smem, smem, vmem, hbm, hbm, hbm, hbm, hbm],
        out_specs=(vmem, vmem, vmem),
        scratch_shapes=[
            pltpu.VMEM((chunks, n, 4, rows, LANES), bf16),
            pltpu.VMEM((chunks, n, 4, rows, LANES), bf16),
            pltpu.VMEM((rows, cols), bf16),
            pltpu.VMEM((n, 2, heads, rows), f32),
            pltpu.VMEM((n, 2, heads, rows), f32),
            pltpu.VMEM((2, heads, group_rows), f32),
            pltpu.VMEM((n, rows, LANES), f32),
            pltpu.VMEM((n, rows, LANES), f32),
            pltpu.VMEM((n, rows, group_rows), f32),
            pltpu.VMEM((group_rows, LANES), bf16),
            pltpu.VMEM((group_rows, LANES), bf16),
            pltpu.VMEM((group_rows, LANES), f32),
            pltpu.VMEM((chunks, n, 3, rows, LANES), bf16),
            pltpu.VMEM((blocks, 3, rows, LANES), bf16),
            pltpu.VMEM((blocks, 3, rows, LANES), bf16),
            pltpu.VMEM((blocks, 3, rows, LANES), bf16),
            dma((chunks, n)),
            dma((chunks, n)),
            dma((n,)),
            dma((n,)),
            dma((chunks, n)),
            dma((chunks, n)),
            dma((blocks,)),
            dma((blocks,)),
            dma((blocks,)),
            dma((blocks,)),
            dma((chunks, 4, n)),
            dma,
        ],
        compiler_params=pltpu.CompilerParams(collective_id=0, has_side_effects=True),
    )(freq, sample_len, plan_offset, log_norm.T, query_in, key_in, value_in, grad_out, fwd_out)


def solution(mesh):
    tokens = P(("grp", "ulys"), None)
    in_specs = (tokens,) * 6 + (P("grp", None), P("grp", None))
    body = functools.partial(per_device, mesh.shape["ulys"], mesh.shape["grp"])
    return jax.shard_map(
        body, mesh=mesh, in_specs=in_specs, out_specs=(tokens,) * 3, check_vma=False
    )
```

profile of v0, /device:TPU:3, one launch (start us, length us, event | category | flops | bytes accessed | tf_op | source)
XLA Modules:
  0.0 69.4 jit_solution(5994275526208131061)
XLA Ops:
  0.6 66.4 %shard_map.112 = (bf16[128,2048]{1,0:T(8,128)(2,1)S(1)}, bf16[128,2048]{1,0:T(8,128)(2,1)S(1)}, bf16[128,2048]{1,0:T(8,128)(2,1)S(1)}) custom-call(f32[1,128]{1,0:T(1,128)} %constant.2.clone.freq_ref, s32[1,4]{1,0:T(1,128)} %len_ref.1, s32[1,4]{1,0:T(1,128)} %plan_ref.1, f32[32,128]{1,0:T(8,128)} %bitcast.1, bf16[128,2048]{1,0:T(8,128)(2,1)} %q_ref.1, ...), custom_call_target="tpu_custom_call" | custom-call | tf_op jit(solution)/shard_map/pallas_call | solution.py:348
  67.0 0.8 %copy.15 = bf16[128,2048]{1,0:T(8,128)(2,1)} copy(bf16[128,2048]{1,0:T(8,128)(2,1)S(1)} %get-tuple-element.3) | data formatting | bytes 1048576
  67.8 0.8 %copy.16 = bf16[128,2048]{1,0:T(8,128)(2,1)} copy(bf16[128,2048]{1,0:T(8,128)(2,1)S(1)} %get-tuple-element.4) | data formatting | bytes 1048576
  68.6 0.8 %copy.17 = bf16[128,2048]{1,0:T(8,128)(2,1)} copy(bf16[128,2048]{1,0:T(8,128)(2,1)S(1)} %get-tuple-element.5) | data formatting | bytes 1048576
where the time goes:
time: 70.6 us; the launch traced here: 69.4 us
  Pallas kernels  66.4 us (94%)
  local copies, waits for them, and re-layouts  2.38 us (3%)
    pallas_call x1, Pallas kernels, per_device(): pl.pallas_call(functools.partial(kernel, n, groups, head_dim), out_shape=...  66.4 us
    unnamed x3, local copies, waits for them, and re-layouts  2.38 us

commit v1 on v0

--- a/solution.py
+++ b/solution.py
@@ -384,10 +384,505 @@
     )(freq, sample_len, plan_offset, log_norm.T, query_in, key_in, value_in, grad_out, fwd_out)
 
 
+CORES = 2
+LAG = 2
+INPUTS = 4
+GRADS = 3
+
+
+def spread(x, slots, half):
+    groups = LANES // half
+    turned = [x] + [pltpu.roll(x, half * j, 1) for j in range(1, groups)]
+    group = lax.broadcasted_iota(jnp.int32, x.shape, 1) // half
+    out = []
+    for s in range(slots):
+        y = turned[(groups - 1 - s) % groups]
+        for j in range(groups - 1):
+            y = jnp.where(group == j, turned[(j - s) % groups], y)
+        out.append(y)
+    return out
+
+
+def halves_kernel(
+    groups, head_dim, lag,
+    freq_ref, len_ref, plan_ref, lse_ref, q_ref, k_ref, v_ref, d_ref, f_ref,
+    oq_ref, ok_ref, ov_ref,
+    in_buf, stage, f_vm, y_in, y_out, stat_oth, stat_in, stat, cos_t, sin_t, bias,
+    qs, kr, dd, dsb, km, acc, grad, keep, home, pair, relay,
+    l_sem, f_sem, c_send, c_recv, st_send, st_recv, d_send, y_send, y_recv,
+    x_send, x_recv, h_send, h_recv, z_send, z_recv,
+):
+    f32, bf16 = jnp.float32, jnp.bfloat16
+    g = lax.axis_index("grp")
+    me = lax.axis_index("ulys")
+    heads_all, rows = lse_ref.shape
+    heads = heads_all // CORES
+    chunks = in_buf.shape[0]
+    width = chunks * LANES
+    per_chunk = LANES // head_dim
+    half = head_dim // 2
+    slots = CORES + 1
+    span = slots * rows
+    inputs = (q_ref, k_ref, v_ref, d_ref)
+
+    c = lax.rem(me, CORES)
+    yc = me // CORES
+    far, near = yc, 1 - yc
+    sib = me + 1 - 2 * c
+    opp_base = CORES * (1 - yc)
+    mate_base = CORES * yc
+    is_near, is_far = c == near, c == far
+
+    even = lax.rem(g, 2) == 0
+    partner = jnp.where(even, g + 1, g - 1)
+    up, down = g + 2, g - 2
+    has_up, has_down = up < groups, down >= 0
+    z_to = jnp.where(even, up, down)
+    has_to = jnp.where(even, has_up, has_down)
+    has_from = jnp.where(even, has_down, has_up)
+
+    barrier = pltpu.get_barrier_semaphore()
+    peers = [(g, sib)] + [(g, opp_base + o) for o in range(CORES)]
+    peers += [(partner, mate_base + o) for o in range(CORES)]
+    for peer in peers:
+        pl.semaphore_signal(barrier, inc=1, device_id=peer, device_id_type=MESH)
+
+    @pl.when(has_up)
+    def _():
+        pl.semaphore_signal(barrier, inc=1, device_id=(up, me), device_id_type=MESH)
+
+    @pl.when(has_down)
+    def _():
+        pl.semaphore_signal(barrier, inc=1, device_id=(down, me), device_id_type=MESH)
+
+    def load(p, t, other):
+        w = 1 - c if other else c
+        dst = stage.at[p, t] if other else in_buf.at[p, c, t]
+        return pltpu.make_async_copy(
+            inputs[t].at[:, pl.ds(pl.multiple_of(w * width + p * LANES, LANES), LANES)],
+            dst, l_sem.at[p, t, int(other)],
+        )
+
+    def load_f(other):
+        w = 1 - c if other else c
+        return pltpu.make_async_copy(
+            f_ref.at[:, pl.ds(pl.multiple_of(w * width, LANES), width)], f_vm.at[int(other)], f_sem.at[int(other)],
+        )
+
+    def remote(src, dst, send, recv, to):
+        return pltpu.make_async_remote_copy(
+            src_ref=src, dst_ref=dst, send_sem=send, recv_sem=recv, device_id=to, device_id_type=MESH,
+        )
+
+    def core_copy(p, slot):
+        return remote(stage.at[p], in_buf.at[p, slot], c_send.at[p], c_recv.at[p], (g, sib))
+
+    def first_copy(m, other):
+        src = stage.at[m] if other else in_buf.at[m, c]
+        to = 1 - c if other else c
+        return remote(src, y_in.at[m], d_send.at[m, int(other)], y_recv.at[m], (g, opp_base + to))
+
+    def y_copy(p):
+        return remote(y_out.at[p], y_in.at[p + lag], y_send.at[p], y_recv.at[p + lag], (g, opp_base + c))
+
+    def y_arrival(m):
+        return remote(y_out.at[0], y_in.at[m], y_send.at[0], y_recv.at[m], (g, opp_base + c))
+
+    def y_last_arrival(m):
+        keep_to = pl.ds(0, GRADS)
+        return remote(
+            y_out.at[0, keep_to], y_in.at[m, keep_to], y_send.at[0], y_recv.at[m], (g, opp_base + c)
+        )
+
+    def y_last(p):
+        return remote(
+            y_out.at[p, pl.ds(0, GRADS)], y_in.at[p + lag, pl.ds(0, GRADS)],
+            y_send.at[p], y_recv.at[p + lag], (g, opp_base + c),
+        )
+
+    def stat_core(slot):
+        return remote(stat_oth, stat_in.at[slot], st_send.at[0], st_recv.at[slot], (g, sib))
+
+    def stat_far(other):
+        src = stat_oth if other else stat_in.at[c]
+        to = 1 - c if other else c
+        return remote(src, stat_in.at[CORES], st_send.at[1 + int(other)], st_recv.at[CORES], (g, opp_base + to))
+
+    def x_copy(p, slot, kind, h):
+        return remote(
+            grad.at[p, slot], pair.at[h, p], x_send.at[kind, p], x_recv.at[h, p], (partner, mate_base + slot),
+        )
+
+    def home_copy(p, h):
+        return remote(grad.at[p, 1 - c], home.at[h, p], h_send.at[p], h_recv.at[p], (g, sib))
+
+    def z_copy(h, p):
+        return remote(pair.at[h, p], relay.at[h, p], z_send.at[h, p], z_recv.at[h, p], (z_to, me))
+
+    for t in range(INPUTS):
+        for other in (False, True):
+            load(0, t, other).start()
+    load_f(False).start()
+    load_f(True).start()
+    for p in range(1, chunks):
+        for t in reversed(range(INPUTS)):
+            for other in (False, True):
+                load(p, t, other).start()
+
+    lengths = [len_ref[0, s] for s in range(len_ref.shape[1])]
+    ends = []
+    for s, length in enumerate(lengths):
+        ends.append(length if s == 0 else ends[-1] + length)
+    cut = sum(jnp.where(e <= CORES * rows, n, 0) for e, n in zip(ends, lengths))
+    ship = jnp.where(cut >= rows, 1 - yc, yc)
+    lane = lax.broadcasted_iota(jnp.int32, (rows, LANES), 1)
+    low = lax.rem(lane, head_dim) < half
+    shipping = jnp.full((rows, LANES), ship, jnp.int32) == 1
+
+    def segments(index):
+        return sum((index >= e).astype(jnp.int32) for e in ends)
+
+    other_at = (2 - yc) * rows
+    own_at = mate_base * rows
+    group = lane // half
+    row = lax.broadcasted_iota(jnp.int32, (rows, LANES), 0)
+    row = jnp.where(group < CORES, own_at + group * rows, other_at) + row
+    start = sum(jnp.where(row >= e, n, 0) for e, n in zip(ends, lengths))
+    angle = (row - start).astype(f32) * freq_ref[...]
+    for s, value in enumerate(spread(jnp.cos(angle), slots, half)):
+        cos_t[s] = value
+    for s, value in enumerate(spread(jnp.sin(angle), slots, half)):
+        sin_t[s] = jnp.where(low, -value, value)
+
+    col = lax.broadcasted_iota(jnp.int32, (1, span), 1)
+    own_col = col < CORES * rows
+    seg_i = segments(jnp.where(own_col, own_at + col, other_at - CORES * rows + col))
+    sent = jnp.full((1, span), ship, jnp.int32) == 1
+    for s in range(slots):
+        at = own_at + s * rows if s < CORES else other_at
+        seg_j = segments(lax.broadcasted_iota(jnp.int32, (rows, 1), 0) + at)
+        if s < CORES:
+            same = seg_j == jnp.where(own_col, seg_i, jnp.where(sent, -1, seg_i))
+        else:
+            same = seg_j == jnp.where(own_col, jnp.where(sent, -1, seg_i), -1)
+        bias[s] = jnp.where(same, 0.0, -1e30)
+
+    for t in range(INPUTS):
+        for other in (False, True):
+            load(0, t, other).wait()
+    pl.semaphore_wait(barrier, len(peers) + has_up.astype(jnp.int32) + has_down.astype(jnp.int32))
+
+    @pl.when(is_near)
+    def _():
+        first_copy(0, False).start()
+        first_copy(0, True).start()
+
+    core_copy(0, c).start()
+
+    for p in range(1, chunks):
+        for other in (False, True):
+            load(p, INPUTS - 1, other).wait()
+    for other in (False, True):
+        load_f(other).wait()
+    owner = lax.broadcasted_iota(jnp.int32, (heads, width), 1) - head_dim * lax.broadcasted_iota(
+        jnp.int32, (heads, width), 0
+    )
+    pick = jnp.where((owner >= 0) & (owner < head_dim), 1.0, 0.0).astype(bf16)
+    for other in (True, False):
+        if other:
+            tiles = [stage[p, INPUTS - 1] for p in range(chunks)]
+        else:
+            tiles = [in_buf[p, c, INPUTS - 1] for p in range(chunks)]
+        prod = jnp.concatenate(tiles, axis=1).astype(f32) * f_vm[int(other)].astype(f32)
+        high = prod.astype(bf16)
+        rest = (prod - high.astype(f32)).astype(bf16)
+        delta = lax.dot_general(pick, high, NT, preferred_element_type=f32)
+        delta += lax.dot_general(pick, rest, NT, preferred_element_type=f32)
+        w = 1 - c if other else c
+        lse = lse_ref[pl.ds(pl.multiple_of(w * heads, heads), heads), :]
+        if other:
+            stat_oth[0] = lse
+            stat_oth[1] = delta
+        else:
+            stat_in[c, 0] = lse
+            stat_in[c, 1] = delta
+    stat_core(c).start()
+
+    @pl.when(is_near)
+    def _():
+        stat_far(False).start()
+        stat_far(True).start()
+
+    for p in range(1, chunks):
+        for t in range(INPUTS - 1):
+            for other in (False, True):
+                load(p, t, other).wait()
+        if p < lag:
+            @pl.when(is_near)
+            def _(p=p):
+                first_copy(p, False).start()
+                first_copy(p, True).start()
+
+        core_copy(p, c).start()
+
+    @pl.when(jnp.logical_not(has_from))
+    def _():
+        relay[...] = jnp.zeros_like(relay)
+
+    stat_core(1 - c).wait_recv()
+    stat_far(False).wait_recv()
+    for s in range(slots):
+        stat[:, :, s * rows:(s + 1) * rows] = stat_in[s]
+    for p in range(min(lag, chunks)):
+        core_copy(p, 1 - c).wait_recv()
+
+    head_of = lax.broadcasted_iota(jnp.int32, (1, LANES), 1) // head_dim
+
+    def turn_back(x, s):
+        return x * cos_t[s] - swap_halves(x, low, half) * sin_t[s]
+
+    def compute(p):
+        for s in range(slots):
+            at = slice(s * rows, (s + 1) * rows)
+
+            def take(t):
+                return in_buf[p, s, t] if s < CORES else y_in[p, t]
+
+            for t, out in ((0, qs), (1, kr)):
+                x = take(t).astype(f32)
+                y = (x * cos_t[s] + swap_halves(x, low, half) * sin_t[s]).astype(bf16)
+                out[at, :] = y * 0.125 if t == 0 else y
+            dd[at, :] = take(3)
+        shares = []
+        for s in range(slots):
+            k_blk = kr[s * rows:(s + 1) * rows, :]
+            v_blk = in_buf[p, s, 2] if s < CORES else y_in[p, 2]
+            q_all, d_all = qs[...], dd[...]
+            gv = jnp.zeros((rows, LANES), f32)
+            gk = jnp.zeros((rows, LANES), f32)
+            for a in range(per_chunk):
+                mine = head_of == a
+                q_a = jnp.where(mine, q_all, 0)
+                d_a = jnp.where(mine, d_all, 0)
+                at = slice((s * per_chunk + a) * rows, (s * per_chunk + a + 1) * rows)
+                km[at, :] = jnp.where(mine, k_blk, 0)
+                h = pl.ds(p * per_chunk + a, 1)
+                score = lax.dot_general(k_blk, q_a, NT, preferred_element_type=f32)
+                prob = jnp.exp(score + bias[s] - stat[0, h, :])
+                dp = lax.dot_general(v_blk, d_a, NT, preferred_element_type=f32)
+                ds = (prob * (dp - stat[1, h, :])).astype(bf16)
+                gv += jnp.dot(prob.astype(bf16), d_a, preferred_element_type=f32)
+                gk += jnp.dot(ds, q_a, preferred_element_type=f32)
+                dsb[at, :] = ds
+            gk = turn_back(gk, s)
+            if s < CORES:
+                acc[s, 1] = gk
+                acc[s, 2] = gv
+            else:
+                shares = [gk, gv]
+        dq = lax.dot_general(dsb[...], km[...], TN, preferred_element_type=f32) * 0.125
+        for s in range(slots):
+            part = turn_back(dq[s * rows:(s + 1) * rows, :], s)
+            if s < CORES:
+                acc[s, 0] = part
+            else:
+                shares = [part] + shares
+        m = jnp.minimum(p + lag, chunks - 1)
+        for t in range(GRADS):
+            y_out[p, t] = jnp.where(shipping, in_buf[m, near, t], shares[t].astype(bf16))
+        y_out[p, 3] = in_buf[m, near, 3]
+
+        @pl.when(p + lag < chunks)
+        def _():
+            y_copy(p).start()
+
+        @pl.when(p + lag >= chunks)
+        def _():
+            y_last(p).start()
+
+        for t in range(GRADS):
+            grad[p, far, t] = acc[far, t].astype(bf16)
+            keep[p, t] = acc[near, t]
+
+    def hand_on(p, slot, kind):
+        x_copy(p, slot, kind, c).start()
+
+        @pl.when(c == slot)
+        def _():
+            home[c, p] = grad[p, slot]
+
+        @pl.when(c != slot)
+        def _():
+            home_copy(p, c).start()
+
+    offset = jnp.full((rows, LANES), plan_ref[0, me], jnp.int32)
+    toward = jnp.where(even, 1, -1)
+    stay, beside = offset == 0, offset == toward
+    wait_x = jnp.where(is_far, 1, lag + 1)
+
+    def deliver(q):
+        home_copy(q, 1 - c).wait_recv()
+        for h in range(CORES):
+            @pl.when(has_from)
+            def _(h=h):
+                z_copy(h, q).wait_recv()
+
+            at = pl.ds(pl.multiple_of((h * chunks + q) * LANES, LANES), LANES)
+            for t, out in enumerate((oq_ref, ok_ref, ov_ref)):
+                out[:, at] = jnp.where(stay, home[h, q, t], jnp.where(beside, pair[h, q, t], relay[h, q, t]))
+
+    def step(p, carry):
+        @pl.when(p + lag < chunks)
+        def _():
+            core_copy(p + lag, 1 - c).wait_recv()
+
+        @pl.when(p < chunks)
+        def _():
+            y_arrival(p).wait_recv()
+
+        @pl.when((p >= chunks) & (p < chunks + lag))
+        def _():
+            y_last_arrival(p).wait_recv()
+
+        @pl.when((p >= lag) & (p < chunks + lag))
+        def _():
+            q = p - lag
+            for t in range(GRADS):
+                got = jnp.where(shipping, y_in[p, t].astype(f32), 0.0)
+                grad[q, near, t] = (keep[q, t] + got).astype(bf16)
+            hand_on(q, near, 1)
+
+        @pl.when(p < chunks)
+        def _():
+            compute(p)
+            hand_on(p, far, 0)
+
+        at = p - wait_x
+
+        @pl.when((at >= 0) & (at < chunks))
+        def _():
+            for h in range(CORES):
+                x_copy(at, c, 0, h).wait_recv()
+
+                @pl.when(has_to)
+                def _(h=h):
+                    z_copy(h, at).start()
+
+        done = at - 2
+
+        @pl.when((done >= 0) & (done < chunks))
+        def _():
+            deliver(done)
+
+        return carry
+
+    lax.fori_loop(0, chunks + lag + 3, step, 0)
+
+    stat_core(c).wait_send()
+
+    @pl.when(is_near)
+    def _():
+        for other in (False, True):
+            stat_far(other).wait_send()
+            for m in range(lag):
+                first_copy(m, other).wait_send()
+
+    def drain(p, carry):
+        core_copy(p, c).wait_send()
+
+        @pl.when(p + lag < chunks)
+        def _():
+            y_copy(p).wait_send()
+
+        @pl.when(p + lag >= chunks)
+        def _():
+            y_last(p).wait_send()
+
+        x_copy(p, far, 0, c).wait_send()
+        x_copy(p, near, 1, c).wait_send()
+        home_copy(p, c).wait_send()
+
+        @pl.when(has_to)
+        def _():
+            for h in range(CORES):
+                z_copy(h, p).wait_send()
+
+        return carry
+
+    lax.fori_loop(0, chunks, drain, 0)
+
+
+def per_device_halves(n, groups, query_in, key_in, value_in, grad_out, fwd_out, log_norm, sample_len, plan_offset):
+    rows, cols = query_in.shape
+    heads_all = log_norm.shape[1]
+    head_dim = cols // heads_all
+    half = head_dim // 2
+    chunks = cols // CORES // LANES
+    heads = heads_all // CORES
+    slots = CORES + 1
+    per_chunk = LANES // head_dim
+    lag = min(LAG, chunks)
+    freq = np.power(10000.0, -np.arange(half) / half).astype(np.float32)
+    freq = jnp.asarray(np.tile(freq, LANES // half)[None, :])
+    bf16, f32 = jnp.bfloat16, jnp.float32
+    vmem = pl.BlockSpec(memory_space=pltpu.VMEM)
+    smem = pl.BlockSpec(memory_space=pltpu.SMEM)
+    hbm = pl.BlockSpec(memory_space=pl.ANY)
+    dma = pltpu.SemaphoreType.DMA
+    return pl.pallas_call(
+        functools.partial(halves_kernel, groups, head_dim, lag),
+        out_shape=(pltpu.VMEM((rows, cols), bf16),) * 3,
+        in_specs=[vmem, smem, smem, vmem, hbm, hbm, hbm, hbm, hbm],
+        out_specs=(vmem, vmem, vmem),
+        scratch_shapes=[
+            pltpu.VMEM((chunks, CORES, INPUTS, rows, LANES), bf16),
+            pltpu.VMEM((chunks, INPUTS, rows, LANES), bf16),
+            pltpu.VMEM((CORES, rows, cols // CORES), bf16),
+            pltpu.VMEM((chunks + lag, INPUTS, rows, LANES), bf16),
+            pltpu.VMEM((chunks, INPUTS, rows, LANES), bf16),
+            pltpu.VMEM((2, heads, rows), f32),
+            pltpu.VMEM((slots, 2, heads, rows), f32),
+            pltpu.VMEM((2, heads, slots * rows), f32),
+            pltpu.VMEM((slots, rows, LANES), f32),
+            pltpu.VMEM((slots, rows, LANES), f32),
+            pltpu.VMEM((slots, rows, slots * rows), f32),
+            pltpu.VMEM((slots * rows, LANES), bf16),
+            pltpu.VMEM((slots * rows, LANES), bf16),
+            pltpu.VMEM((slots * rows, LANES), bf16),
+            pltpu.VMEM((slots * per_chunk * rows, slots * rows), bf16),
+            pltpu.VMEM((slots * per_chunk * rows, LANES), bf16),
+            pltpu.VMEM((CORES, GRADS, rows, LANES), f32),
+            pltpu.VMEM((chunks, CORES, GRADS, rows, LANES), bf16),
+            pltpu.VMEM((chunks, GRADS, rows, LANES), f32),
+            pltpu.VMEM((CORES, chunks, GRADS, rows, LANES), bf16),
+            pltpu.VMEM((CORES, chunks, GRADS, rows, LANES), bf16),
+            pltpu.VMEM((CORES, chunks, GRADS, rows, LANES), bf16),
+            dma((chunks, INPUTS, 2)),
+            dma((2,)),
+            dma((chunks,)),
+            dma((chunks,)),
+            dma((3,)),
+            dma((slots,)),
+            dma((lag, 2)),
+            dma((chunks,)),
+            dma((chunks + lag,)),
+            dma((2, chunks)),
+            dma((CORES, chunks)),
+            dma((chunks,)),
+            dma((chunks,)),
+            dma((CORES, chunks)),
+            dma((CORES, chunks)),
+        ],
+        compiler_params=pltpu.CompilerParams(collective_id=0, has_side_effects=True),
+    )(freq, sample_len, plan_offset, log_norm.T, query_in, key_in, value_in, grad_out, fwd_out)
+
+
 def solution(mesh):
     tokens = P(("grp", "ulys"), None)
     in_specs = (tokens,) * 6 + (P("grp", None), P("grp", None))
-    body = functools.partial(per_device, mesh.shape["ulys"], mesh.shape["grp"])
+    n = mesh.shape["ulys"]
+    two_chips = n == 2 * CORES
+    body = functools.partial(per_device_halves if two_chips else per_device, n, mesh.shape["grp"])
     return jax.shard_map(
         body, mesh=mesh, in_specs=in_specs, out_specs=(tokens,) * 3, check_vma=False
     )

time: 70.6 us -> 57 us (0.81); the launches traced: 69.4 us -> 56.8 us
  Pallas kernels: 66.4 us -> 53.7 us
    pallas_call x1, Pallas kernels: 66.4 us -> 53.7 us  [per_device_halves(): pl.pallas_call(functools.partial(halves_kernel, groups, head_dim, lag), o...]
where the time goes in v1:
time: 57 us; the launch traced here: 56.8 us
  Pallas kernels  53.7 us (94%)
  local copies, waits for them, and re-layouts  2.38 us (4%)
  between operations  0.64 us (1%)
    pallas_call x1, Pallas kernels, per_device_halves(): pl.pallas_call(functools.partial(halves_kernel, groups, head_dim, lag), o...  53.7 us
    unnamed x3, local copies, waits for them, and re-layouts  2.38 us

profile of v1, /device:TPU:3, one launch (start us, length us, event | category | flops | bytes accessed | tf_op | source)
XLA Modules:
  0.0 56.8 jit_solution(15268928808546339244)
XLA Ops:
  0.6 53.7 %shard_map.112 = (bf16[128,2048]{1,0:T(8,128)(2,1)S(1)}, bf16[128,2048]{1,0:T(8,128)(2,1)S(1)}, bf16[128,2048]{1,0:T(8,128)(2,1)S(1)}) custom-call(f32[1,128]{1,0:T(1,128)} %constant.2.clone.freq_ref, s32[1,4]{1,0:T(1,128)} %len_ref.1, s32[1,4]{1,0:T(1,128)} %plan_ref.1, f32[32,128]{1,0:T(8,128)} %bitcast.1, bf16[128,2048]{1,0:T(8,128)(2,1)} %q_ref.1, ...), custom_call_target="tpu_custom_call" | custom-call | tf_op jit(solution)/shard_map/pallas_call | solution.py:832
  54.4 0.8 %copy.15 = bf16[128,2048]{1,0:T(8,128)(2,1)} copy(bf16[128,2048]{1,0:T(8,128)(2,1)S(1)} %get-tuple-element.3) | data formatting | bytes 1048576
  55.2 0.8 %copy.16 = bf16[128,2048]{1,0:T(8,128)(2,1)} copy(bf16[128,2048]{1,0:T(8,128)(2,1)S(1)} %get-tuple-element.4) | data formatting | bytes 1048576
  56.0 0.8 %copy.17 = bf16[128,2048]{1,0:T(8,128)(2,1)} copy(bf16[128,2048]{1,0:T(8,128)(2,1)S(1)} %get-tuple-element.5) | data formatting | bytes 1048576

commit v2 on v1

--- a/solution.py
+++ b/solution.py
@@ -386,6 +386,8 @@
 
 CORES = 2
 LAG = 2
+LATE = 2
+RELAY = 2
 INPUTS = 4
 GRADS = 3
 
@@ -404,18 +406,18 @@
 
 
 def halves_kernel(
-    groups, head_dim, lag,
-    freq_ref, len_ref, plan_ref, lse_ref, q_ref, k_ref, v_ref, d_ref, f_ref,
+    groups, head_dim, lag, early,
+    freq_hbm, len_hbm, plan_hbm, lse_hbm, q_ref, k_ref, v_ref, d_ref, f_ref,
     oq_ref, ok_ref, ov_ref,
-    in_buf, stage, f_vm, y_in, y_out, stat_oth, stat_in, stat, cos_t, sin_t, bias,
-    qs, kr, dd, dsb, km, acc, grad, keep, home, pair, relay,
-    l_sem, f_sem, c_send, c_recv, st_send, st_recv, d_send, y_send, y_recv,
+    freq_ref, len_ref, plan_ref, lse_ref, in_buf, stage, f_vm, y_in, y_out, stat_oth, stat_in, stat, cos_t, sin_t, bias,
+    qs, kr, dd, dsb, km, acc, grad, keep, home, pair, relay, mix,
+    s_sem, l_sem, f_sem, c_send, c_recv, st_send, st_recv, d_send, y_send, y_recv,
     x_send, x_recv, h_send, h_recv, z_send, z_recv,
 ):
     f32, bf16 = jnp.float32, jnp.bfloat16
     g = lax.axis_index("grp")
     me = lax.axis_index("ulys")
-    heads_all, rows = lse_ref.shape
+    heads_all, rows = lse_hbm.shape
     heads = heads_all // CORES
     chunks = in_buf.shape[0]
     width = chunks * LANES
@@ -438,6 +440,7 @@
     up, down = g + 2, g - 2
     has_up, has_down = up < groups, down >= 0
     z_to = jnp.where(even, up, down)
+    z_back = jnp.where(even, down, up)
     has_to = jnp.where(even, has_up, has_down)
     has_from = jnp.where(even, has_down, has_up)
 
@@ -516,18 +519,37 @@
     def home_copy(p, h):
         return remote(grad.at[p, 1 - c], home.at[h, p], h_send.at[p], h_recv.at[p], (g, sib))
 
+    def x_late(h, p):
+        return remote(mix.at[h, p - early], pair.at[h, p], x_send.at[h, p], x_recv.at[h, p], (partner, me))
+
+    def z_late(h, p):
+        return remote(home.at[h, p], relay.at[h, p], z_send.at[h, p], z_recv.at[h, p], (z_back, me))
+
     def z_copy(h, p):
         return remote(pair.at[h, p], relay.at[h, p], z_send.at[h, p], z_recv.at[h, p], (z_to, me))
 
+    small = [
+        pltpu.make_async_copy(src, dst, s_sem.at[i])
+        for i, (src, dst) in enumerate(
+            ((len_hbm, len_ref), (freq_hbm, freq_ref), (plan_hbm, plan_ref), (lse_hbm, lse_ref))
+        )
+    ]
+    small[0].start()
+    small[1].start()
     for t in range(INPUTS):
         for other in (False, True):
             load(0, t, other).start()
     load_f(False).start()
     load_f(True).start()
-    for p in range(1, chunks):
-        for t in reversed(range(INPUTS)):
+    for t in reversed(range(INPUTS)):
+        for p in range(1, chunks):
             for other in (False, True):
                 load(p, t, other).start()
+        if t == INPUTS - 1:
+            small[2].start()
+            small[3].start()
+    small[0].wait()
+    small[1].wait()
 
     lengths = [len_ref[0, s] for s in range(len_ref.shape[1])]
     ends = []
@@ -575,9 +597,10 @@
     @pl.when(is_near)
     def _():
         first_copy(0, False).start()
-        first_copy(0, True).start()
 
     core_copy(0, c).start()
+    small[2].wait()
+    small[3].wait()
 
     for p in range(1, chunks):
         for other in (False, True):
@@ -612,6 +635,7 @@
     def _():
         stat_far(False).start()
         stat_far(True).start()
+        first_copy(0, True).start()
 
     for p in range(1, chunks):
         for t in range(INPUTS - 1):
@@ -625,9 +649,11 @@
 
         core_copy(p, c).start()
 
-    @pl.when(jnp.logical_not(has_from))
-    def _():
-        relay[...] = jnp.zeros_like(relay)
+    for idle, chosen in ((has_from, slice(0, early)), (has_to, slice(early, chunks))):
+        @pl.when(jnp.logical_not(idle))
+        def _(chosen=chosen):
+            for h in range(CORES):
+                relay[h, chosen] = jnp.zeros_like(relay[h, chosen])
 
     stat_core(1 - c).wait_recv()
     stat_far(False).wait_recv()
@@ -705,7 +731,9 @@
             keep[p, t] = acc[near, t]
 
     def hand_on(p, slot, kind):
-        x_copy(p, slot, kind, c).start()
+        @pl.when(p < early)
+        def _():
+            x_copy(p, slot, kind, c).start()
 
         @pl.when(c == slot)
         def _():
@@ -718,18 +746,26 @@
     offset = jnp.full((rows, LANES), plan_ref[0, me], jnp.int32)
     toward = jnp.where(even, 1, -1)
     stay, beside = offset == 0, offset == toward
-    wait_x = jnp.where(is_far, 1, lag + 1)
+    base = jnp.where(is_far, 0, lag)
 
     def deliver(q):
-        home_copy(q, 1 - c).wait_recv()
+        @pl.when(q < early)
+        def _():
+            home_copy(q, 1 - c).wait_recv()
+
         for h in range(CORES):
-            @pl.when(has_from)
+            @pl.when((q < early) & has_from)
             def _(h=h):
                 z_copy(h, q).wait_recv()
 
+            @pl.when(q >= early)
+            def _(h=h):
+                x_late(h, q).wait_recv()
+
+            near_by = beside | (jnp.full((rows, LANES), q, jnp.int32) >= early)
             at = pl.ds(pl.multiple_of((h * chunks + q) * LANES, LANES), LANES)
             for t, out in enumerate((oq_ref, ok_ref, ov_ref)):
-                out[:, at] = jnp.where(stay, home[h, q, t], jnp.where(beside, pair[h, q, t], relay[h, q, t]))
+                out[:, at] = jnp.where(stay, home[h, q, t], jnp.where(near_by, pair[h, q, t], relay[h, q, t]))
 
     def step(p, carry):
         @pl.when(p + lag < chunks)
@@ -757,18 +793,42 @@
             compute(p)
             hand_on(p, far, 0)
 
-        at = p - wait_x
-
-        @pl.when((at >= 0) & (at < chunks))
+        give = p - base - jnp.where(is_far, 1, 0)
+
+        @pl.when((give >= early) & (give < chunks))
+        def _():
+            home_copy(give, 1 - c).wait_recv()
+
+            @pl.when(has_from)
+            def _():
+                for h in range(CORES):
+                    z_late(h, give).start()
+
+        cross = give - 1
+
+        @pl.when((cross >= early) & (cross < chunks))
         def _():
             for h in range(CORES):
-                x_copy(at, c, 0, h).wait_recv()
-
                 @pl.when(has_to)
                 def _(h=h):
-                    z_copy(h, at).start()
-
-        done = at - 2
+                    z_late(h, cross).wait_recv()
+
+                for t in range(GRADS):
+                    mix[h, cross - early, t] = jnp.where(beside, home[h, cross, t], relay[h, cross, t])
+                x_late(h, cross).start()
+
+        pass_on = p - base - RELAY
+
+        @pl.when((pass_on >= 0) & (pass_on < early))
+        def _():
+            for h in range(CORES):
+                x_copy(pass_on, c, 0, h).wait_recv()
+
+                @pl.when(has_to)
+                def _(h=h):
+                    z_copy(h, pass_on).start()
+
+        done = pass_on - 2
 
         @pl.when((done >= 0) & (done < chunks))
         def _():
@@ -776,7 +836,7 @@
 
         return carry
 
-    lax.fori_loop(0, chunks + lag + 3, step, 0)
+    lax.fori_loop(0, chunks + lag + RELAY + 2, step, 0)
 
     stat_core(c).wait_send()
 
@@ -798,14 +858,27 @@
         def _():
             y_last(p).wait_send()
 
-        x_copy(p, far, 0, c).wait_send()
-        x_copy(p, near, 1, c).wait_send()
         home_copy(p, c).wait_send()
 
-        @pl.when(has_to)
+        @pl.when(p < early)
+        def _():
+            x_copy(p, far, 0, c).wait_send()
+            x_copy(p, near, 1, c).wait_send()
+
+        @pl.when((p < early) & has_to)
         def _():
             for h in range(CORES):
                 z_copy(h, p).wait_send()
+
+        @pl.when(p >= early)
+        def _():
+            for h in range(CORES):
+                x_late(h, p).wait_send()
+
+        @pl.when((p >= early) & has_from)
+        def _():
+            for h in range(CORES):
+                z_late(h, p).wait_send()
 
         return carry
 
@@ -822,19 +895,23 @@
     slots = CORES + 1
     per_chunk = LANES // head_dim
     lag = min(LAG, chunks)
+    early = max(chunks - LATE, 1)
     freq = np.power(10000.0, -np.arange(half) / half).astype(np.float32)
     freq = jnp.asarray(np.tile(freq, LANES // half)[None, :])
     bf16, f32 = jnp.bfloat16, jnp.float32
     vmem = pl.BlockSpec(memory_space=pltpu.VMEM)
-    smem = pl.BlockSpec(memory_space=pltpu.SMEM)
     hbm = pl.BlockSpec(memory_space=pl.ANY)
     dma = pltpu.SemaphoreType.DMA
     return pl.pallas_call(
-        functools.partial(halves_kernel, groups, head_dim, lag),
+        functools.partial(halves_kernel, groups, head_dim, lag, early),
         out_shape=(pltpu.VMEM((rows, cols), bf16),) * 3,
-        in_specs=[vmem, smem, smem, vmem, hbm, hbm, hbm, hbm, hbm],
+        in_specs=[hbm] * 9,
         out_specs=(vmem, vmem, vmem),
         scratch_shapes=[
+            pltpu.VMEM((1, LANES), f32),
+            pltpu.SMEM(sample_len.shape, jnp.int32),
+            pltpu.SMEM(plan_offset.shape, jnp.int32),
+            pltpu.VMEM((heads_all, rows), f32),
             pltpu.VMEM((chunks, CORES, INPUTS, rows, LANES), bf16),
             pltpu.VMEM((chunks, INPUTS, rows, LANES), bf16),
             pltpu.VMEM((CORES, rows, cols // CORES), bf16),
@@ -857,6 +934,8 @@
             pltpu.VMEM((CORES, chunks, GRADS, rows, LANES), bf16),
             pltpu.VMEM((CORES, chunks, GRADS, rows, LANES), bf16),
             pltpu.VMEM((CORES, chunks, GRADS, rows, LANES), bf16),
+            pltpu.VMEM((CORES, chunks - early, GRADS, rows, LANES), bf16),
+            dma((4,)),
             dma((chunks, INPUTS, 2)),
             dma((2,)),
             dma((chunks,)),

time: 57 us -> 53.6 us (0.940)
  Pallas kernels: 53.7 us -> 50.3 us
    pallas_call x1, Pallas kernels: 53.7 us -> 50.3 us  [per_device_halves(): pl.pallas_call(functools.partial(halves_kernel, groups, head_dim, lag, ea...]
where the time goes in v2:
time: 53.6 us; the launch traced here: 53.3 us
  Pallas kernels  50.3 us (94%)
  local copies, waits for them, and re-layouts  2.38 us (4%)
  between operations  0.64 us (1%)
    pallas_call x1, Pallas kernels, per_device_halves(): pl.pallas_call(functools.partial(halves_kernel, groups, head_dim, lag, ea...  50.3 us
    unnamed x3, local copies, waits for them, and re-layouts  2.38 us

profile of v2, /device:TPU:3, one launch (start us, length us, event | category | flops | bytes accessed | tf_op | source)
XLA Modules:
  0.0 53.3 jit_solution(16920538381657547393)
XLA Ops:
  0.6 50.3 %shard_map.112 = (bf16[128,2048]{1,0:T(8,128)(2,1)S(1)}, bf16[128,2048]{1,0:T(8,128)(2,1)S(1)}, bf16[128,2048]{1,0:T(8,128)(2,1)S(1)}) custom-call(f32[1,128]{1,0:T(1,128)} %constant.2.clone.freq_hbm, s32[1,4]{1,0:T(1,128)} %len_hbm.1, s32[1,4]{1,0:T(1,128)} %plan_hbm.1, f32[32,128]{1,0:T(8,128)} %bitcast.1, bf16[128,2048]{1,0:T(8,128)(2,1)} %q_ref.1, ...), custom_call_target="tpu_custom_call" | custom-call | tf_op jit(solution)/shard_map/pallas_call | solution.py:905
  51.0 0.8 %copy.15 = bf16[128,2048]{1,0:T(8,128)(2,1)} copy(bf16[128,2048]{1,0:T(8,128)(2,1)S(1)} %get-tuple-element.3) | data formatting | bytes 1048576
  51.8 0.8 %copy.16 = bf16[128,2048]{1,0:T(8,128)(2,1)} copy(bf16[128,2048]{1,0:T(8,128)(2,1)S(1)} %get-tuple-element.4) | data formatting | bytes 1048576
  52.6 0.8 %copy.17 = bf16[128,2048]{1,0:T(8,128)(2,1)} copy(bf16[128,2048]{1,0:T(8,128)(2,1)S(1)} %get-tuple-element.5) | data formatting | bytes 1048576
